TPU v7x, 512 devices: a whole 4x4x16 slice. The times are simulated.
512 devices in a mesh: dp: 32 (over y_lo, z), gx: 2 (over core), gy: 8 (over x, y_hi).
Axes of the slice: x: 4, y: 4 (y_hi: 2, y_lo: 2; y = y_hi * 2 + y_lo), z: 16, core: 2. Of those that a mesh axis runs over, the one named last changes fastest.
Arguments:
- field: float32 [32, 64, 1024], P('dp', 'gx', 'gy'), may hold values from -6 to 6
- cotangent: float32 [32, 64, 1024], P('dp', 'gx', 'gy')
- checker: int32 [64, 1024], P('gx', 'gy'), may hold values from 0 to 1, as said below
- weight_in: float32 [3, 3, 32], replicated, may hold values from -2 to 2
- weight_mid: bfloat16 [3, 3, 32, 32], replicated, may hold values from -0.375 to 0.375
- weight_head: bfloat16 [2, 32], replicated, may hold values from -1 to 1
- prior_grads: float32 [32, 2, 8, 23, 9568], P('dp', 'gx', 'gy')
Outputs:
- coupled: float32 [32, 64, 1024], P('dp', 'gx', 'gy')
- field_grad: float32 [32, 64, 1024], P('dp', 'gx', 'gy')
- summed_grads: float32 [24, 9568], replicated
Inputs may be any that keep to these rules, and one draw needn't show every extreme that they name: Each row alternates along the columns: checker[i, j] = (j + p[i]) mod 2, with a parity p[i] of its own for every row i.
All inputs are finite; a program needn't handle non-finite values.
Results may differ from a plain program's by a relative error of at most 0.0034.
Values may be sent and summed in bfloat16 or wider, within the bound.
A program may use at most 64 MiB of HBM per device.

v0:
```python
import math
import jax
import jax.numpy as jnp
from jax import lax
from jax.sharding import PartitionSpec as P


def extended(value, sides, width):
    for axis, dim in sides:
        size, length = (lax.axis_size(axis), value.shape[dim])
        up = [(i, (i + 1) % size) for i in range(size)]
        down = [(j, i) for i, j in up]
        last = lax.slice_in_dim(value, length - width, length, axis=dim)
        initial = lax.slice_in_dim(value, 0, width, axis=dim)
        before = lax.ppermute(last, axis, up)
        after = lax.ppermute(initial, axis, down)
        value = jnp.concatenate([before, value, after], axis=dim)
    return value


def first_conv(padded, weight_in, row_count, col_count):
    total = jnp.zeros((weight_in.shape[2], row_count, col_count), jnp.float32)
    for row_tap in range(3):
        for col_tap in range(3):
            window = padded[row_tap : row_tap + row_count, col_tap : col_tap + col_count]
            total = total + weight_in[row_tap, col_tap][:, None, None] * window[None]
    return total


def on_device(field, cotangent, checker, weight_in, weight_mid, weight_head, prior_grads):
    highest = lax.Precision.HIGHEST
    row_count = field.shape[1]
    col_count = field.shape[2]
    hidden_width = weight_mid.shape[2]
    cell_total = (
        lax.axis_size("dp") * row_count * lax.axis_size("gx") * col_count * lax.axis_size("gy")
    )
    grad_scale = 1.0 / math.sqrt(cell_total)
    values = field[0]
    downstream = cotangent[0]
    frozen = checker.astype(jnp.float32)
    unfrozen = 1.0 - frozen
    masked = frozen * values
    partial_prior = prior_grads.reshape(prior_grads.shape[3], prior_grads.shape[4])
    padded_field = extended(masked, (("gx", 0), ("gy", 1)), 1)
    hidden_one = jnp.tanh(first_conv(padded_field, weight_in, row_count, col_count)).astype(
        jnp.bfloat16
    )
    hidden_pad = extended(hidden_one, (("gx", 1), ("gy", 2)), 1)
    hidden_inner = hidden_pad[:, 1:-1, 1:-1]
    pre_two = jnp.zeros((hidden_width, row_count, col_count), jnp.float32)
    for row_tap in range(3):
        for col_tap in range(3):
            window = hidden_pad[:, row_tap : row_tap + row_count, col_tap : col_tap + col_count]
            pre_two = pre_two + jnp.einsum(
                "oc,cxy->oxy",
                weight_mid[row_tap, col_tap],
                window,
                preferred_element_type=jnp.float32,
            )
    hidden_two = jnp.tanh(pre_two).astype(jnp.bfloat16)
    pair = jnp.einsum("ko,oxy->kxy", weight_head, hidden_two, preferred_element_type=jnp.float32)
    expo = jnp.exp(pair[0])
    coupled = masked + unfrozen * (values * expo + pair[1])
    d_pair = jnp.stack([unfrozen * downstream * values * expo, unfrozen * downstream]).astype(
        jnp.bfloat16
    )
    grad_head = jnp.einsum("kxy,oxy->ko", d_pair, hidden_two, preferred_element_type=jnp.float32)
    d_hidden_two = jnp.einsum(
        "ko,kxy->oxy", weight_head, d_pair, preferred_element_type=jnp.float32
    )
    two_f = hidden_two.astype(jnp.float32)
    d_pre_two = (d_hidden_two * (1.0 - two_f * two_f)).astype(jnp.bfloat16)
    d_two_pad = extended(d_pre_two, (("gx", 1), ("gy", 2)), 1)
    mid_list = []
    d_hidden_one = jnp.zeros((hidden_width, row_count, col_count), jnp.float32)
    for row_tap in range(3):
        for col_tap in range(3):
            window = hidden_pad[:, row_tap : row_tap + row_count, col_tap : col_tap + col_count]
            mid_list.append(
                jnp.einsum("oxy,cxy->oc", d_pre_two, window, preferred_element_type=jnp.float32)
            )
            back_window = d_two_pad[
                :, 2 - row_tap : 2 - row_tap + row_count, 2 - col_tap : 2 - col_tap + col_count
            ]
            d_hidden_one = d_hidden_one + jnp.einsum(
                "oc,oxy->cxy",
                weight_mid[row_tap, col_tap],
                back_window,
                preferred_element_type=jnp.float32,
            )
    one_f = hidden_inner.astype(jnp.float32)
    d_pre_one = d_hidden_one * (1.0 - one_f * one_f)
    in_list = []
    for row_tap in range(3):
        for col_tap in range(3):
            window = padded_field[row_tap : row_tap + row_count, col_tap : col_tap + col_count]
            in_list.append(jnp.einsum("oxy,xy->o", d_pre_one, window, precision=highest))
    d_one_pad = extended(d_pre_one, (("gx", 1), ("gy", 2)), 1)
    d_masked = jnp.zeros((row_count, col_count), jnp.float32)
    for row_tap in range(3):
        for col_tap in range(3):
            back_window = d_one_pad[
                :, 2 - row_tap : 2 - row_tap + row_count, 2 - col_tap : 2 - col_tap + col_count
            ]
            d_masked = d_masked + jnp.einsum(
                "o,oxy->xy", weight_in[row_tap, col_tap], back_window, precision=highest
            )
    field_grad = frozen * downstream + unfrozen * downstream * expo + frozen * d_masked
    layer_grads = (
        jnp.concatenate(
            [jnp.stack(in_list).reshape(-1), jnp.stack(mid_list).reshape(-1), grad_head.reshape(-1)]
        )
        * grad_scale
    )
    stacked = jnp.concatenate([layer_grads[None], partial_prior], axis=0)
    summed_grads = lax.psum(stacked, ("dp", "gx", "gy"))
    return (coupled[None], field_grad[None], summed_grads)


def solution(mesh):
    placed = (
        P("dp", "gx", "gy"),
        P("dp", "gx", "gy"),
        P("gx", "gy"),
        P(),
        P(),
        P(),
        P("dp", "gx", "gy", None, None),
    )
    return jax.shard_map(
        on_device,
        mesh=mesh,
        in_specs=placed,
        out_specs=(P("dp", "gx", "gy"), P("dp", "gx", "gy"), P()),
        check_vma=False,
    )
```

profile of v0, /device:TPU:1, one launch (start us, length us, event | category | flops | bytes accessed | tf_op | source)
XLA Modules:
  0.0 572.6 jit_solution(7181842597088774773)
XLA Ops:
  8.0 8.8 %collective-permute-start = (f32[1,128]{1,0:T(1,128)S(1)}, f32[1,128]{1,0:T(1,128)S(1)}, u32[]{:S(2)}, u32[]{:S(2)}) collective-permute-start(f32[1,128]{1,0:T(1,128)S(1)} %get-tuple-element.38), channel_id=1, source_target_pairs={{0,8},{8,0},{1,9},{9,1},{2,10},{10,2},{3,11},{11,3},{4,12},{12,4},... | collective-permute-start | bytes 1544 | tf_op jit(solution)/shard_map/ppermute | solution.py:15
  16.8 1.9 collective-permute-start.1
  19.6 1.3 copy.81
  20.9 1.9 collective-permute-start.2
  22.9 7.0 %collective-permute-start.3 = (f32[34,1]{1,0:T(8,128)S(1)}, f32[34,1]{1,0:T(8,128)S(1)}, u32[]{:S(2)}, u32[]{:S(2)}) collective-permute-start(f32[34,1]{1,0:T(8,128)S(1)} %get-tuple-element.33), channel_id=1, source_target_pairs={{1,0},{2,1},{3,2},{4,3},{5,4},{6,5},{7,6},{0,7},{9,8},{10,9},{11,1... | collective-permute-start | bytes 416 | tf_op jit(solution)/shard_map/ppermute | solution.py:16
  31.3 3.5 collective-permute-start.4
  34.9 1.9 collective-permute-start.5
  38.1 1.9 collective-permute-start.6
  40.0 7.5 %collective-permute-start.7 = (bf16[32,34,1]{2,0,1:T(8,128)(2,1)S(1)}, bf16[32,34,1]{2,0,1:T(8,128)(2,1)S(1)}, u32[]{:S(2)}, u32[]{:S(2)}) collective-permute-start(bf16[32,34,1]{2,0,1:T(8,128)(2,1)S(1)} %get-tuple-element.16), channel_id=1, source_target_pairs={{1,0},{2,1},{3,2},{4,3},{5,4},{6,5},{7,6},{0,7},{9,8},{10,9},{11,1... | collective-permute-start | bytes 6536 | tf_op jit(solution)/shard_map/ppermute | solution.py:16
  48.0 4.6 collective-permute-done.6
  52.7 4.9 collective-permute-done.7
  63.3 2.9 collective-permute-start.9
  66.1 1.9 collective-permute-start.8
  69.4 5.6 collective-permute-start.10
  75.0 1.9 collective-permute-start.11
  77.5 3.5 collective-permute-done.10
  81.0 7.4 %collective-permute-done.11 = bf16[32,34,1]{2,0,1:T(8,128)(2,1)S(1)} collective-permute-done((bf16[32,34,1]{2,0,1:T(8,128)(2,1)S(1)}, bf16[32,34,1]{2,0,1:T(8,128)(2,1)S(1)}, u32[]{:S(2)}, u32[]{:S(2)}) %collective-permute-start.11) | collective-permute-done | bytes 2208 | tf_op jit(solution)/shard_map/ppermute | solution.py:15
  95.8 3.2 collective-permute-start.13
  99.0 1.9 collective-permute-start.12
  103.1 6.0 %collective-permute-start.14 = (f32[32,34,1]{1,0,2:T(8,128)S(1)}, f32[32,34,1]{1,0,2:T(8,128)S(1)}, u32[]{:S(2)}, u32[]{:S(2)}) collective-permute-start(f32[32,34,1]{1,0,2:T(8,128)S(1)} %copy.33), channel_id=1, source_target_pairs={{1,0},{2,1},{3,2},{4,3},{5,4},{6,5},{7,6},{0,7},{9,8},{10,9},{11,1... | collective-permute-start | bytes 13064 | tf_op jit(solution)/shard_map/ppermute | solution.py:16
  109.5 1.9 collective-permute-start.15
  112.8 4.7 collective-permute-done.15
  121.9 441.7 %all-reduce.2.cloned.1.call-done = f32[24,9568]{1,0:T(8,128)} async-done(((f32[24,9568]{1,0:T(8,128)}), f32[24,9568]{1,0:T(8,128)}) %all-reduce.2.cloned.1.call-update) | async-done | bytes 918544 | tf_op jit(solution)/shard_map/psum | solution.py:117
  563.6 2.2 copy.91
  (109 shorter events, 28.0 us)
Async XLA Ops:
  7.2 52.4 %copy-start = (bf16[2,32]{1,0:T(2,128)(2,1)S(1)}, bf16[2,32]{1,0:T(2,128)(2,1)}, u32[]{:S(2)}) copy-start(bf16[2,32]{1,0:T(2,128)(2,1)} %param.12) | copy-start | bytes 388
  7.2 556.4 %all-reduce.2.cloned.1.call-start = ((), (), s32[]{:S(2)}) async-start(), calls=%async_computation | async-start | bytes 1843200 | tf_op jit(solution)/shard_map/psum | solution.py:117
  8.0 12.9 %collective-permute-start = (f32[1,128]{1,0:T(1,128)S(1)}, f32[1,128]{1,0:T(1,128)S(1)}, u32[]{:S(2)}, u32[]{:S(2)}) collective-permute-start(f32[1,128]{1,0:T(1,128)S(1)} %get-tuple-element.38), channel_id=1, source_target_pairs={{0,8},{8,0},{1,9},{9,1},{2,10},{10,2},{3,11},{11,3},{4,12},{12,4},... | collective-permute-start | bytes 1544 | tf_op jit(solution)/shard_map/ppermute | solution.py:15
  16.8 4.1 collective-permute-start.1
  19.5 17.2 %copy-start.1 = (bf16[3,3,32,32]{3,2,1,0:T(8,128)(2,1)S(1)}, bf16[3,3,32,32]{3,2,1,0:T(8,128)(2,1)}, u32[]{:S(2)}) copy-start(bf16[3,3,32,32]{3,2,1,0:T(8,128)(2,1)} %param.11) | copy-start | bytes 55300
  20.9 8.9 %collective-permute-start.2 = (f32[34,1]{1,0:T(8,128)S(1)}, f32[34,1]{1,0:T(8,128)S(1)}, u32[]{:S(2)}, u32[]{:S(2)}) collective-permute-start(f32[34,1]{1,0:T(8,128)S(1)} %get-tuple-element.32), channel_id=1, source_target_pairs={{0,1},{1,2},{2,3},{3,4},{4,5},{5,6},{6,7},{7,0},{8,9},{9,10},{10,1... | collective-permute-start | bytes 416 | tf_op jit(solution)/shard_map/ppermute | solution.py:15
  22.9 7.9 %collective-permute-start.3 = (f32[34,1]{1,0:T(8,128)S(1)}, f32[34,1]{1,0:T(8,128)S(1)}, u32[]{:S(2)}, u32[]{:S(2)}) collective-permute-start(f32[34,1]{1,0:T(8,128)S(1)} %get-tuple-element.33), channel_id=1, source_target_pairs={{1,0},{2,1},{3,2},{4,3},{5,4},{6,5},{7,6},{0,7},{9,8},{10,9},{11,1... | collective-permute-start | bytes 416 | tf_op jit(solution)/shard_map/ppermute | solution.py:16
  31.3 5.7 collective-permute-start.4
  34.9 3.1 collective-permute-start.5
  38.1 14.5 %collective-permute-start.6 = (bf16[32,34,1]{2,0,1:T(8,128)(2,1)S(1)}, bf16[32,34,1]{2,0,1:T(8,128)(2,1)S(1)}, u32[]{:S(2)}, u32[]{:S(2)}) collective-permute-start(bf16[32,34,1]{2,0,1:T(8,128)(2,1)S(1)} %get-tuple-element.15), channel_id=1, source_target_pairs={{0,1},{1,2},{2,3},{3,4},{4,5},{5,6},{6,7},{7,0},{8,9},{9,10},{10,1... | collective-permute-start | bytes 6536 | tf_op jit(solution)/shard_map/ppermute | solution.py:15
  40.0 17.5 %collective-permute-start.7 = (bf16[32,34,1]{2,0,1:T(8,128)(2,1)S(1)}, bf16[32,34,1]{2,0,1:T(8,128)(2,1)S(1)}, u32[]{:S(2)}, u32[]{:S(2)}) collective-permute-start(bf16[32,34,1]{2,0,1:T(8,128)(2,1)S(1)} %get-tuple-element.16), channel_id=1, source_target_pairs={{1,0},{2,1},{3,2},{4,3},{5,4},{6,5},{7,6},{0,7},{9,8},{10,9},{11,1... | collective-permute-start | bytes 6536 | tf_op jit(solution)/shard_map/ppermute | solution.py:16
  59.2 0.7 copy-start.2
  59.2 0.7 copy-start.4
  59.2 0.7 copy-start.5
  63.3 5.2 collective-permute-start.9
  66.1 3.1 collective-permute-start.8
  69.4 11.6 %collective-permute-start.10 = (bf16[32,34,1]{2,0,1:T(8,128)(2,1)S(1)}, bf16[32,34,1]{2,0,1:T(8,128)(2,1)S(1)}, u32[]{:S(2)}, u32[]{:S(2)}) collective-permute-start(bf16[32,34,1]{2,0,1:T(8,128)(2,1)S(1)} %get-tuple-element.11), channel_id=1, source_target_pairs={{1,0},{2,1},{3,2},{4,3},{5,4},{6,5},{7,6},{0,7},{9,8},{10,9},{11,1... | collective-permute-start | bytes 6536 | tf_op jit(solution)/shard_map/ppermute | solution.py:16
  75.0 13.3 %collective-permute-start.11 = (bf16[32,34,1]{2,0,1:T(8,128)(2,1)S(1)}, bf16[32,34,1]{2,0,1:T(8,128)(2,1)S(1)}, u32[]{:S(2)}, u32[]{:S(2)}) collective-permute-start(bf16[32,34,1]{2,0,1:T(8,128)(2,1)S(1)} %get-tuple-element.12), channel_id=1, source_target_pairs={{0,1},{1,2},{2,3},{3,4},{4,5},{5,6},{6,7},{7,0},{8,9},{9,10},{10,1... | collective-permute-start | bytes 6536 | tf_op jit(solution)/shard_map/ppermute | solution.py:15
  95.4 6.6 %copy-start.3 = (f32[3,3,32]{2,1,0:T(4,128)S(1)}, f32[3,3,32]{2,1,0:T(4,128)}, u32[]{:S(2)}) copy-start(f32[3,3,32]{2,1,0:T(4,128)} %param.10) | copy-start | bytes 3460
  95.8 6.6 %collective-permute-start.13 = (f32[32,1,128]{2,0,1:T(8,128)S(1)}, f32[32,1,128]{2,0,1:T(8,128)S(1)}, u32[]{:S(2)}, u32[]{:S(2)}) collective-permute-start(f32[32,1,128]{2,0,1:T(8,128)S(1)} %get-tuple-element.8), channel_id=1, source_target_pairs={{8,0},{0,8},{9,1},{1,9},{10,2},{2,10},{11,3},{3,11},{12,4},{4,12},... | collective-permute-start | bytes 49160 | tf_op jit(solution)/shard_map/ppermute | solution.py:16
  99.0 3.4 collective-permute-start.12
  103.1 9.1 %collective-permute-start.14 = (f32[32,34,1]{1,0,2:T(8,128)S(1)}, f32[32,34,1]{1,0,2:T(8,128)S(1)}, u32[]{:S(2)}, u32[]{:S(2)}) collective-permute-start(f32[32,34,1]{1,0,2:T(8,128)S(1)} %copy.33), channel_id=1, source_target_pairs={{1,0},{2,1},{3,2},{4,3},{5,4},{6,5},{7,6},{0,7},{9,8},{10,9},{11,1... | collective-permute-start | bytes 13064 | tf_op jit(solution)/shard_map/ppermute | solution.py:16
  109.5 8.1 %collective-permute-start.15 = (f32[32,34,1]{1,0,2:T(8,128)S(1)}, f32[32,34,1]{1,0,2:T(8,128)S(1)}, u32[]{:S(2)}, u32[]{:S(2)}) collective-permute-start(f32[32,34,1]{1,0,2:T(8,128)S(1)} %copy.35), channel_id=1, source_target_pairs={{0,1},{1,2},{2,3},{3,4},{4,5},{5,6},{6,7},{7,0},{8,9},{9,10},{10,1... | collective-permute-start | bytes 13064 | tf_op jit(solution)/shard_map/ppermute | solution.py:15
Sparse Core Ops, SparseCore 0:
  102.5 461.0 all-reduce.1
where the time goes:
time: 573 us
  waiting for transfers between devices  469 us (82%)
  starting transfers between devices  59.9 us (10%)
  matrix products  16.1 us (3%)
  between operations  14.6 us (3%)
  local copies, waits for them, and re-layouts  7.8 us (1%)
    psum x1, waiting for transfers between devices, on_device(): summed_grads = lax.psum(stacked, ('dp', 'gx', 'gy'))  442 us
    ppermute x8, starting transfers between devices, extended(): after = lax.ppermute(initial, axis, down)  36 us
    ppermute x8, starting transfers between devices, extended(): before = lax.ppermute(last, axis, up)  23.8 us
    ppermute x8, waiting for transfers between devices, extended(): before = lax.ppermute(last, axis, up)  17.5 us
  transfers between devices with their start and end apart: 17, of which 9 were waited for; matrix products, arithmetic and copies ran while one was open for 2% of the time, Pallas kernels for 0%

commit v1 on v0

--- a/solution.py
+++ b/solution.py
@@ -114,7 +114,7 @@
         * grad_scale
     )
     stacked = jnp.concatenate([layer_grads[None], partial_prior], axis=0)
-    summed_grads = lax.psum(stacked, ("dp", "gx", "gy"))
+    summed_grads = lax.psum(lax.psum(stacked, ("gx", "gy")), "dp")
     return (coupled[None], field_grad[None], summed_grads)
 
 

time: 573 us -> 532 us (0.928)
  the two profiles are of different devices: /device:TPU:1 before, /device:TPU:2 now
where the time goes in v1:
time: 532 us; the launch traced here: 531 us
  waiting for transfers between devices  435 us (82%)
  starting transfers between devices  50.6 us (10%)
  matrix products  16.1 us (3%)
  between operations  14.6 us (3%)
  local copies, waits for them, and re-layouts  8.54 us (2%)
  other arithmetic  5.95 us (1%)
    psum x2, waiting for transfers between devices, on_device(): summed_grads = lax.psum(lax.psum(stacked, ('gx', 'gy')), 'dp')  404 us
    ppermute x8, starting transfers between devices, extended(): after = lax.ppermute(initial, axis, down)  28.7 us
    ppermute x8, starting transfers between devices, extended(): before = lax.ppermute(last, axis, up)  21.6 us
    ppermute x8, waiting for transfers between devices, extended(): before = lax.ppermute(last, axis, up)  19.8 us
    ppermute x8, waiting for transfers between devices, extended(): after = lax.ppermute(initial, axis, down)  11.3 us
  transfers between devices with their start and end apart: 18, of which 10 were waited for; matrix products, arithmetic and copies ran while one was open for 3% of the time, Pallas kernels for 0%

profile of v1, /device:TPU:2, one launch (start us, length us, event | category | flops | bytes accessed | tf_op | source)
XLA Modules:
  0.0 530.8 jit_solution(15385120740991326324)
XLA Ops:
  8.0 1.9 collective-permute-start
  9.9 2.4 collective-permute-start.1
  14.6 5.1 collective-permute-start.2
  19.7 3.1 collective-permute-start.3
  22.8 4.0 collective-permute-done.3
  27.4 1.9 collective-permute-start.4
  29.4 2.4 collective-permute-start.5
  32.8 4.1 collective-permute-start.6
  36.8 4.2 collective-permute-start.7
  41.4 7.8 %collective-permute-done.6 = bf16[32,34,1]{2,0,1:T(8,128)(2,1)S(1)} collective-permute-done((bf16[32,34,1]{2,0,1:T(8,128)(2,1)S(1)}, bf16[32,34,1]{2,0,1:T(8,128)(2,1)S(1)}, u32[]{:S(2)}, u32[]{:S(2)}) %collective-permute-start.6) | collective-permute-done | bytes 2208 | tf_op jit(solution)/shard_map/ppermute | solution.py:15
  49.2 2.7 collective-permute-done.7
  57.7 1.9 collective-permute-start.9
  59.6 2.4 collective-permute-start.8
  63.0 6.5 %collective-permute-start.10 = (bf16[32,34,1]{2,0,1:T(8,128)(2,1)S(1)}, bf16[32,34,1]{2,0,1:T(8,128)(2,1)S(1)}, u32[]{:S(2)}, u32[]{:S(2)}) collective-permute-start(bf16[32,34,1]{2,0,1:T(8,128)(2,1)S(1)} %get-tuple-element.11), channel_id=1, source_target_pairs={{1,0},{2,1},{3,2},{4,3},{5,4},{6,5},{7,6},{0,7},{9,8},{10,9},{11,1... | collective-permute-start | bytes 6536 | tf_op jit(solution)/shard_map/ppermute | solution.py:16
  69.5 1.9 collective-permute-start.11
  72.0 3.9 collective-permute-done.10
  75.9 6.5 %collective-permute-done.11 = bf16[32,34,1]{2,0,1:T(8,128)(2,1)S(1)} collective-permute-done((bf16[32,34,1]{2,0,1:T(8,128)(2,1)S(1)}, bf16[32,34,1]{2,0,1:T(8,128)(2,1)S(1)}, u32[]{:S(2)}, u32[]{:S(2)}) %collective-permute-start.11) | collective-permute-done | bytes 2208 | tf_op jit(solution)/shard_map/ppermute | solution.py:15
  89.9 1.9 collective-permute-start.13
  91.8 2.4 collective-permute-start.12
  96.6 6.2 %collective-permute-start.14 = (f32[32,34,1]{1,0,2:T(8,128)S(1)}, f32[32,34,1]{1,0,2:T(8,128)S(1)}, u32[]{:S(2)}, u32[]{:S(2)}) collective-permute-start(f32[32,34,1]{1,0,2:T(8,128)S(1)} %copy.33), channel_id=1, source_target_pairs={{1,0},{2,1},{3,2},{4,3},{5,4},{6,5},{7,6},{0,7},{9,8},{10,9},{11,1... | collective-permute-start | bytes 13064 | tf_op jit(solution)/shard_map/ppermute | solution.py:16
  106.6 5.1 collective-permute-done.15
  116.0 145.8 %all-reduce.3.cloned.1.call-done = f32[24,9568]{1,0:T(8,128)} async-done(((f32[24,9568]{1,0:T(8,128)}), f32[24,9568]{1,0:T(8,128)}) %all-reduce.3.cloned.1.call-update) | async-done | bytes 918544 | tf_op jit(solution)/shard_map/psum | solution.py:117
  263.7 258.1 %all-reduce.5.cloned.1.call-done = f32[24,9568]{1,0:T(8,128)} async-done(((f32[24,9568]{1,0:T(8,128)}), f32[24,9568]{1,0:T(8,128)}) %all-reduce.5.cloned.1.call-update) | async-done | bytes 918544 | tf_op jit(solution)/shard_map/psum | solution.py:117
  521.8 2.2 copy.92
  (112 shorter events, 31.7 us)
Async XLA Ops:
  7.2 46.8 %copy-start = (bf16[2,32]{1,0:T(2,128)(2,1)S(1)}, bf16[2,32]{1,0:T(2,128)(2,1)}, u32[]{:S(2)}) copy-start(bf16[2,32]{1,0:T(2,128)(2,1)} %param.12) | copy-start | bytes 388
  7.2 254.6 %all-reduce.3.cloned.1.call-start = ((), (), s32[]{:S(2)}) async-start(), calls=%async_computation | async-start | bytes 1843200 | tf_op jit(solution)/shard_map/psum | solution.py:117
  8.0 6.5 %collective-permute-start = (f32[1,128]{1,0:T(1,128)S(1)}, f32[1,128]{1,0:T(1,128)S(1)}, u32[]{:S(2)}, u32[]{:S(2)}) collective-permute-start(f32[1,128]{1,0:T(1,128)S(1)} %get-tuple-element.38), channel_id=1, source_target_pairs={{0,8},{8,0},{1,9},{9,1},{2,10},{10,2},{3,11},{11,3},{4,12},{12,4},... | collective-permute-start | bytes 1544 | tf_op jit(solution)/shard_map/ppermute | solution.py:15
  9.9 4.6 collective-permute-start.1
  13.2 18.6 %copy-start.1 = (bf16[3,3,32,32]{3,2,1,0:T(8,128)(2,1)S(1)}, bf16[3,3,32,32]{3,2,1,0:T(8,128)(2,1)}, u32[]{:S(2)}) copy-start(bf16[3,3,32,32]{3,2,1,0:T(8,128)(2,1)} %param.11) | copy-start | bytes 55300
  14.6 8.3 %collective-permute-start.2 = (f32[34,1]{1,0:T(8,128)S(1)}, f32[34,1]{1,0:T(8,128)S(1)}, u32[]{:S(2)}, u32[]{:S(2)}) collective-permute-start(f32[34,1]{1,0:T(8,128)S(1)} %get-tuple-element.32), channel_id=1, source_target_pairs={{0,1},{1,2},{2,3},{3,4},{4,5},{5,6},{6,7},{7,0},{8,9},{9,10},{10,1... | collective-permute-start | bytes 416 | tf_op jit(solution)/shard_map/ppermute | solution.py:15
  19.7 7.2 %collective-permute-start.3 = (f32[34,1]{1,0:T(8,128)S(1)}, f32[34,1]{1,0:T(8,128)S(1)}, u32[]{:S(2)}, u32[]{:S(2)}) collective-permute-start(f32[34,1]{1,0:T(8,128)S(1)} %get-tuple-element.33), channel_id=1, source_target_pairs={{1,0},{2,1},{3,2},{4,3},{5,4},{6,5},{7,6},{0,7},{9,8},{10,9},{11,1... | collective-permute-start | bytes 416 | tf_op jit(solution)/shard_map/ppermute | solution.py:16
  27.4 4.6 collective-permute-start.4
  29.4 3.2 collective-permute-start.5
  32.8 16.4 %collective-permute-start.6 = (bf16[32,34,1]{2,0,1:T(8,128)(2,1)S(1)}, bf16[32,34,1]{2,0,1:T(8,128)(2,1)S(1)}, u32[]{:S(2)}, u32[]{:S(2)}) collective-permute-start(bf16[32,34,1]{2,0,1:T(8,128)(2,1)S(1)} %get-tuple-element.15), channel_id=1, source_target_pairs={{0,1},{1,2},{2,3},{3,4},{4,5},{5,6},{6,7},{7,0},{8,9},{9,10},{10,1... | collective-permute-start | bytes 6536 | tf_op jit(solution)/shard_map/ppermute | solution.py:15
  36.8 15.1 %collective-permute-start.7 = (bf16[32,34,1]{2,0,1:T(8,128)(2,1)S(1)}, bf16[32,34,1]{2,0,1:T(8,128)(2,1)S(1)}, u32[]{:S(2)}, u32[]{:S(2)}) collective-permute-start(bf16[32,34,1]{2,0,1:T(8,128)(2,1)S(1)} %get-tuple-element.16), channel_id=1, source_target_pairs={{1,0},{2,1},{3,2},{4,3},{5,4},{6,5},{7,6},{0,7},{9,8},{10,9},{11,1... | collective-permute-start | bytes 6536 | tf_op jit(solution)/shard_map/ppermute | solution.py:16
  53.6 0.7 copy-start.2
  53.6 0.7 copy-start.4
  53.6 0.7 copy-start.5
  57.7 4.8 collective-permute-start.9
  59.6 3.2 collective-permute-start.8
  63.0 12.9 %collective-permute-start.10 = (bf16[32,34,1]{2,0,1:T(8,128)(2,1)S(1)}, bf16[32,34,1]{2,0,1:T(8,128)(2,1)S(1)}, u32[]{:S(2)}, u32[]{:S(2)}) collective-permute-start(bf16[32,34,1]{2,0,1:T(8,128)(2,1)S(1)} %get-tuple-element.11), channel_id=1, source_target_pairs={{1,0},{2,1},{3,2},{4,3},{5,4},{6,5},{7,6},{0,7},{9,8},{10,9},{11,1... | collective-permute-start | bytes 6536 | tf_op jit(solution)/shard_map/ppermute | solution.py:16
  69.5 12.9 %collective-permute-start.11 = (bf16[32,34,1]{2,0,1:T(8,128)(2,1)S(1)}, bf16[32,34,1]{2,0,1:T(8,128)(2,1)S(1)}, u32[]{:S(2)}, u32[]{:S(2)}) collective-permute-start(bf16[32,34,1]{2,0,1:T(8,128)(2,1)S(1)} %get-tuple-element.12), channel_id=1, source_target_pairs={{0,1},{1,2},{2,3},{3,4},{4,5},{5,6},{6,7},{7,0},{8,9},{9,10},{10,1... | collective-permute-start | bytes 6536 | tf_op jit(solution)/shard_map/ppermute | solution.py:15
  89.5 5.8 %copy-start.3 = (f32[3,3,32]{2,1,0:T(4,128)S(1)}, f32[3,3,32]{2,1,0:T(4,128)}, u32[]{:S(2)}) copy-start(f32[3,3,32]{2,1,0:T(4,128)} %param.10) | copy-start | bytes 3460
  89.9 6.0 %collective-permute-start.13 = (f32[32,1,128]{2,0,1:T(8,128)S(1)}, f32[32,1,128]{2,0,1:T(8,128)S(1)}, u32[]{:S(2)}, u32[]{:S(2)}) collective-permute-start(f32[32,1,128]{2,0,1:T(8,128)S(1)} %get-tuple-element.8), channel_id=1, source_target_pairs={{8,0},{0,8},{9,1},{1,9},{10,2},{2,10},{11,3},{3,11},{12,4},{4,12},... | collective-permute-start | bytes 49160 | tf_op jit(solution)/shard_map/ppermute | solution.py:16
  91.8 4.1 collective-permute-start.12
  95.7 426.1 %all-reduce.5.cloned.1.call-start = ((), (), s32[]{:S(2)}) async-start(), calls=%async_computation.1 | async-start | bytes 1843200 | tf_op jit(solution)/shard_map/psum | solution.py:117
  96.6 9.4 %collective-permute-start.14 = (f32[32,34,1]{1,0,2:T(8,128)S(1)}, f32[32,34,1]{1,0,2:T(8,128)S(1)}, u32[]{:S(2)}, u32[]{:S(2)}) collective-permute-start(f32[32,34,1]{1,0,2:T(8,128)S(1)} %copy.33), channel_id=1, source_target_pairs={{1,0},{2,1},{3,2},{4,3},{5,4},{6,5},{7,6},{0,7},{9,8},{10,9},{11,1... | collective-permute-start | bytes 13064 | tf_op jit(solution)/shard_map/ppermute | solution.py:16
  103.3 8.5 %collective-permute-start.15 = (f32[32,34,1]{1,0,2:T(8,128)S(1)}, f32[32,34,1]{1,0,2:T(8,128)S(1)}, u32[]{:S(2)}, u32[]{:S(2)}) collective-permute-start(f32[32,34,1]{1,0,2:T(8,128)S(1)} %copy.35), channel_id=1, source_target_pairs={{0,1},{1,2},{2,3},{3,4},{4,5},{5,6},{6,7},{7,0},{8,9},{9,10},{10,1... | collective-permute-start | bytes 13064 | tf_op jit(solution)/shard_map/ppermute | solution.py:15
Sparse Core Ops, SparseCore 0:
  95.8 165.9 all-reduce.2
  264.9 256.7 all-reduce.4
